TPU v7x, 256 devices: a whole 4x4x8 slice. The times are simulated.
256 devices in a mesh: shard: 8 (over y, core), tensor: 4 (over x), section: 8 (over z).
Axes of the slice: x: 4, y: 4, z: 8, core: 2. Of those that a mesh axis runs over, the one named last changes fastest.
Arguments:
- normed_inputs: bfloat16 [65536, 4096], P(('shard', 'section')), may hold values from -320 to 320
- projection_cotangent: bfloat16 [65536, 2, 1024], P(('shard', 'section'), None, 'tensor'), may hold values from -1 to 1
- small_partials: bfloat16 [64, 10, 4096], P(('shard', 'section'), None, 'tensor'), may hold values from -2000 to 2000
- master_weights: float32 [4096, 2, 1024], P(('shard', 'section'), None, 'tensor'), may hold values from -4 to 4
- first_moment: float32 [4096, 2, 1024], P(('shard', 'section'), None, 'tensor'), may hold values from -3 to 3
- second_moment: float32 [4096, 2, 1024], P(('shard', 'section'), None, 'tensor'), may hold values from 0.05 to 1
- small_master: float32 [10, 4096], P(None, 'tensor'), may hold values from -4 to 4
- small_first: float32 [10, 4096], P(None, 'tensor'), may hold values from -3 to 3
- small_second: float32 [10, 4096], P(None, 'tensor'), may hold values from 0.05 to 1
Outputs:
- updated_master: float32 [4096, 2, 1024], P(('shard', 'section'), None, 'tensor')
- updated_first: float32 [4096, 2, 1024], P(('shard', 'section'), None, 'tensor')
- updated_second: float32 [4096, 2, 1024], P(('shard', 'section'), None, 'tensor')
- gathered_weights: bfloat16 [4096, 2, 1024], P(None, None, 'tensor')
- small_updated_master: float32 [10, 4096], P(None, 'tensor')
- small_updated_first: float32 [10, 4096], P(None, 'tensor')
- small_updated_second: float32 [10, 4096], P(None, 'tensor')
- small_weights: bfloat16 [10, 4096], P(None, 'tensor')
All inputs are finite; a program needn't handle non-finite values.
Results may differ from a plain program's by a relative error of at most 0.0015.
Values may be sent and summed in bfloat16 or wider, within the bound.
A program may use at most 64 MiB of HBM per device.

v0:
```python
import math
import jax
import jax.numpy as jnp
from jax import lax
from jax.sharding import PartitionSpec as P

D = 4096
EXPERTS = 8
STEP = 10
KV_COLS = 1024
SMALL_ROWS = 10
beta_one = 0.9
beta_two = 0.95
learning_rate = 0.01
weight_decay = 0.1
epsilon = 1e-08
clip_factor = 0.5


def adamw(gradient, scale, first, second, master, decay):
    clipped = gradient * scale
    first_new = beta_one * first + (1.0 - beta_one) * clipped
    second_new = beta_two * second + (1.0 - beta_two) * clipped * clipped
    first_hat = first_new / (1.0 - beta_one**STEP)
    second_hat = second_new / (1.0 - beta_two**STEP)
    master_new = master - learning_rate * (
        first_hat / (jnp.sqrt(second_hat) + epsilon) + decay * master
    )
    return (master_new, first_new, second_new)


def body(
    normed_inputs,
    projection_cotangent,
    small_partials,
    master_weights,
    first_moment,
    second_moment,
    small_master,
    small_first,
    small_second,
):
    gradient = lax.psum_scatter(
        jnp.einsum(
            "tf,tjc->fjc", normed_inputs, projection_cotangent, preferred_element_type=jnp.float32
        ),
        ("shard", "section"),
        scatter_dimension=0,
        tiled=True,
    )
    owned_squares = jnp.sum(gradient * gradient)
    local_small = small_partials[0].astype(jnp.float32)
    small_gradient = lax.psum(local_small, ("shard", "section"))
    big_total = lax.psum(owned_squares, ("shard", "tensor", "section"))
    small_total = lax.psum(jnp.sum(small_gradient * small_gradient), "tensor")
    total = big_total + small_total
    limit = clip_factor * math.sqrt(2 * D * KV_COLS + SMALL_ROWS * D)
    scale = jnp.minimum(1.0, limit / (jnp.sqrt(total) + 1e-06))
    master_new, first_new, second_new = adamw(
        gradient, scale, first_moment, second_moment, master_weights, weight_decay
    )
    row_decay = jnp.where(jnp.arange(SMALL_ROWS)[:, None] < EXPERTS, weight_decay, 0.0).astype(
        jnp.float32
    )
    small_master_new, small_first_new, small_second_new = adamw(
        small_gradient, scale, small_first, small_second, small_master, row_decay
    )
    owned_weights = master_new.astype(jnp.bfloat16)
    gathered = lax.all_gather(owned_weights, ("shard", "section"), axis=0, tiled=True)
    return (
        master_new,
        first_new,
        second_new,
        gathered,
        small_master_new,
        small_first_new,
        small_second_new,
        small_master_new.astype(jnp.bfloat16),
    )


def solution(mesh):
    placed = (
        P(("shard", "section"), None),
        P(("shard", "section"), None, "tensor"),
        P(("shard", "section"), None, "tensor"),
        P(("shard", "section"), None, "tensor"),
        P(("shard", "section"), None, "tensor"),
        P(("shard", "section"), None, "tensor"),
        P(None, "tensor"),
        P(None, "tensor"),
        P(None, "tensor"),
    )
    return jax.shard_map(
        body,
        mesh=mesh,
        in_specs=placed,
        out_specs=(
            P(("shard", "section"), None, "tensor"),
            P(("shard", "section"), None, "tensor"),
            P(("shard", "section"), None, "tensor"),
            P(None, None, "tensor"),
            P(None, "tensor"),
            P(None, "tensor"),
            P(None, "tensor"),
            P(None, "tensor"),
        ),
        check_vma=False,
    )
```

profile of v0, /device:TPU:1, one launch (start us, length us, event | category | flops | bytes accessed | tf_op | source)
XLA Modules:
  0.0 454.1 jit_solution(6464595801956574734)
XLA Ops:
  7.2 0.0 copy-start
  7.2 0.0 reduce-scatter.2.cloned.1.call-start
  7.2 1.2 copy-done
  8.4 10.3 %fusion = f32[4096,2,256]{2,0,1:T(8,128)} fusion(bf16[1024,4096]{1,0:T(8,128)(2,1)} %param.9, bf16[1024,2,256]{2,1,0:T(2,128)(2,1)S(1)} %copy-done), kind=kOutput, calls=%fused_computation | convolution fusion | flops 4294967296 | bytes 17825792 | tf_op jit(solution)/shard_map/tf,tjc->fjc/dot_general | solution.py:44
  18.8 0.0 copy-start.4
  18.8 0.0 copy-start.5
  18.8 0.0 copy-start.6
  18.8 0.0 reduce-scatter.2.cloned.1.call-update
  18.8 0.0 all-gather.2.cloned.1.call-start
  18.9 0.6 copy-done.7
  19.5 246.8 %psum.22 = f32[10,1024]{1,0:T(8,128)S(1)} all-reduce(f32[10,1024]{1,0:T(8,128)S(1)} %bitcast_convert_fusion), channel_id=1, replica_groups=mesh['shard'=8,'tensor'=4,'section'=8] {'shard','section'}, use_global_device_ids=true, to_apply=%region_3.0 | all-reduce | flops 10240 | bytes 81920 | tf_op jit(solution)/shard_map/psum | solution.py:53
  266.3 0.6 multiply_reduce_fusion.1
  266.9 1.5 multiply_reduce_fusion
  268.4 9.4 %psum.23 = f32[]{:T(128)} all-reduce(f32[]{:T(128)} %multiply_reduce_fusion.1), channel_id=1, replica_groups=mesh['shard'=8,'tensor'=4,'section'=8] {'tensor'}, use_global_device_ids=true, to_apply=%region_5.0 | all-reduce | flops 1 | bytes 8 | tf_op jit(solution)/shard_map/psum | solution.py:55
  277.9 81.1 %psum.21 = f32[]{:T(128)} all-reduce(f32[]{:T(128)} %multiply_reduce_fusion), channel_id=1, replica_groups=mesh['shard'=8,'tensor'=4,'section'=8] {'shard','tensor','section'}, use_global_device_ids=true, to_apply=%region_2.0 | all-reduce | flops 1 | bytes 8 | tf_op jit(solution)/shard_map/psum | solution.py:54
  360.4 1.7 fusion.8
  362.1 0.0 all-gather.2.cloned.1.call-update
  362.1 0.8 copy.23
  362.9 0.8 copy.24
  363.6 0.8 copy.25
  364.4 0.0 copy-done.5
  364.4 0.7 fusion.6
  365.1 72.0 %all-gather.2.cloned.1.call-done = bf16[4096,2,256]{2,0,1:T(8,128)(2,1)} async-done(((bf16[64,2,256]{2,0,1:T(8,128)(2,1)}), bf16[4096,2,256]{2,0,1:T(8,128)(2,1)}) %all-gather.2.cloned.1.call-update) | async-done | bytes 4194320 | tf_op jit(solution)/shard_map/all_gather | solution.py:69
  437.1 10.1 %copy.26 = bf16[4096,2,256]{2,1,0:T(2,128)(2,1)} copy(bf16[4096,2,256]{2,0,1:T(8,128)(2,1)} %all-gather.2.cloned.1.call-done) | data formatting | bytes 8388608
  (12 shorter events, 0.0 us)
Async XLA Ops:
  7.2 1.2 copy-start
  7.2 259.7 %reduce-scatter.2.cloned.1.call-start = ((), (), s32[]{:S(2)}) async-start(), calls=%async_computation.1 | async-start | bytes 8519680 | tf_op jit(solution)/shard_map/reduce_scatter | solution.py:43
  18.7 0.8 copy-start.7
  18.7 341.7 %copy-start.1 = (f32[64,2,256]{2,1,0:T(2,128)S(1)}, f32[64,2,256]{2,1,0:T(2,128)}, u32[]{:S(2)}) copy-start(f32[64,2,256]{2,1,0:T(2,128)} %param.12) | copy-start | bytes 393220
  18.7 341.7 %copy-start.2 = (f32[64,2,256]{2,1,0:T(2,128)S(1)}, f32[64,2,256]{2,1,0:T(2,128)}, u32[]{:S(2)}) copy-start(f32[64,2,256]{2,1,0:T(2,128)} %param.13) | copy-start | bytes 393220
  18.8 341.7 %copy-start.3 = (f32[64,2,256]{2,1,0:T(2,128)S(1)}, f32[64,2,256]{2,1,0:T(2,128)}, u32[]{:S(2)}) copy-start(f32[64,2,256]{2,1,0:T(2,128)} %param.14) | copy-start | bytes 393220
  18.8 345.6 %copy-start.4 = (f32[10,1024]{1,0:T(8,128)S(1)}, f32[10,1024]{1,0:T(8,128)}, u32[]{:S(2)}) copy-start(f32[10,1024]{1,0:T(8,128)} %param.15) | copy-start | bytes 122884
  18.8 345.6 %copy-start.5 = (f32[10,1024]{1,0:T(8,128)S(1)}, f32[10,1024]{1,0:T(8,128)}, u32[]{:S(2)}) copy-start(f32[10,1024]{1,0:T(8,128)} %param.16) | copy-start | bytes 122884
  18.8 345.6 %copy-start.6 = (f32[10,1024]{1,0:T(8,128)S(1)}, f32[10,1024]{1,0:T(8,128)}, u32[]{:S(2)}) copy-start(f32[10,1024]{1,0:T(8,128)} %param.17) | copy-start | bytes 122884
  18.8 418.3 %all-gather.2.cloned.1.call-start = ((), (), s32[]{:S(2)}) async-start(), calls=%async_computation.2 | async-start | bytes 4259840 | tf_op jit(solution)/shard_map/all_gather | solution.py:69
Sparse Core Ops, SparseCore 0:
  18.9 150.9 reduce-scatter.1
  362.2 74.8 all-gather.1
where the time goes:
time: 455 us; the launch traced here: 454 us
  blocking collectives  337 us (74%)
  waiting for transfers between devices  72 us (16%)
  between operations  15.5 us (3%)
  local copies, waits for them, and re-layouts  14.2 us (3%)
  matrix products  10.3 us (2%)
    psum x1, blocking collectives, body(): small_gradient = lax.psum(local_small, ('shard', 'section'))  247 us
    psum x1, blocking collectives, body(): big_total = lax.psum(owned_squares, ('shard', 'tensor', 'section'))  81.1 us
    all_gather x1, waiting for transfers between devices, body(): lax.all_gather(owned_weights, ('shard', 'section'), axis=0, tiled=True)  72 us
    unnamed x20, local copies, waits for them, and re-layouts  14.2 us
    dot_general x1, matrix products, body(): jnp.einsum('tf,tjc->fjc', normed_inputs, projection_cotangent, preferred_...  10.3 us
    psum x1, blocking collectives, body(): small_total = lax.psum(jnp.sum(small_gradient * small_gradient), 'tensor')  9.45 us
  transfers between devices with their start and end apart: 2, of which 1 were waited for; matrix products, arithmetic and copies ran while one was open for 1% of the time, Pallas kernels for 0%

commit v1 on v0

--- a/solution.py
+++ b/solution.py
@@ -50,7 +50,7 @@
     )
     owned_squares = jnp.sum(gradient * gradient)
     local_small = small_partials[0].astype(jnp.float32)
-    small_gradient = lax.psum(local_small, ("shard", "section"))
+    small_gradient = lax.psum(lax.psum(local_small, "shard"), "section")
     big_total = lax.psum(owned_squares, ("shard", "tensor", "section"))
     small_total = lax.psum(jnp.sum(small_gradient * small_gradient), "tensor")
     total = big_total + small_total

time: 455 us -> 356 us (0.78)
  blocking collectives: 337 us -> 140 us
  waiting for transfers between devices: 72 us -> 171 us
    psum x1 -> x2, blocking collectives: 247 us -> 50.2 us  [body(): small_gradient = lax.psum(lax.psum(local_small, 'shard'), 'section')]
    reduce_scatter x1, waiting for transfers between devices: 0.01 us -> 98.8 us  [body(): lax.psum_scatter(jnp.einsum('tf,tjc->fjc', normed_inputs, projection_cota...]
  transfers between devices with their start and end apart: 2 -> 2, of which waited for: 1 -> 2; matrix products, arithmetic and copies ran while one was open for 1% -> 1% of each run, Pallas kernels for 0% -> 0%
where the time goes in v1:
time: 356 us
  waiting for transfers between devices  171 us (48%)
  blocking collectives  140 us (39%)
  between operations  15.5 us (4%)
  local copies, waits for them, and re-layouts  14.2 us (4%)
  matrix products  10.3 us (3%)
  other arithmetic  4.54 us (1%)
    reduce_scatter x1, waiting for transfers between devices, body(): lax.psum_scatter(jnp.einsum('tf,tjc->fjc', normed_inputs, projection_cota...  98.8 us
    psum x1, blocking collectives, body(): big_total = lax.psum(owned_squares, ('shard', 'tensor', 'section'))  80.5 us
    all_gather x1, waiting for transfers between devices, body(): lax.all_gather(owned_weights, ('shard', 'section'), axis=0, tiled=True)  72.4 us
    psum x2, blocking collectives, body(): small_gradient = lax.psum(lax.psum(local_small, 'shard'), 'section')  50.2 us
    unnamed x20, local copies, waits for them, and re-layouts  14.2 us
    dot_general x1, matrix products, body(): jnp.einsum('tf,tjc->fjc', normed_inputs, projection_cotangent, preferred_...  10.3 us
    psum x1, blocking collectives, body(): small_total = lax.psum(jnp.sum(small_gradient * small_gradient), 'tensor')  9.04 us
  transfers between devices with their start and end apart: 2, of which 2 were waited for; matrix products, arithmetic and copies ran while one was open for 1% of the time, Pallas kernels for 0%

profile of v1, /device:TPU:1, one launch (start us, length us, event | category | flops | bytes accessed | tf_op | source)
XLA Modules:
  0.0 355.7 jit_solution(393781689983362503)
XLA Ops:
  7.2 0.0 copy-start
  7.2 0.0 reduce-scatter.2.cloned.1.call-start
  7.2 1.2 copy-done
  8.4 10.3 %fusion = f32[4096,2,256]{2,0,1:T(8,128)} fusion(bf16[1024,4096]{1,0:T(8,128)(2,1)} %param.9, bf16[1024,2,256]{2,1,0:T(2,128)(2,1)S(1)} %copy-done), kind=kOutput, calls=%fused_computation | convolution fusion | flops 4294967296 | bytes 17825792 | tf_op jit(solution)/shard_map/tf,tjc->fjc/dot_general | solution.py:44
  18.8 0.0 copy-start.5
  18.8 0.0 copy-start.6
  18.8 0.0 reduce-scatter.2.cloned.1.call-update
  18.8 0.0 all-gather.2.cloned.1.call-start
  18.9 0.6 copy-done.7
  19.5 24.3 %psum.29 = f32[10,1024]{1,0:T(8,128)S(1)} all-reduce(f32[10,1024]{1,0:T(8,128)S(1)} %bitcast_convert_fusion), channel_id=1, replica_groups=mesh['shard'=8,'tensor'=4,'section'=8] {'shard'}, use_global_device_ids=true, to_apply=%region_3.0 | all-reduce | flops 10240 | bytes 81920 | tf_op jit(solution)/shard_map/psum | solution.py:53
  43.8 26.0 %psum.30 = f32[10,1024]{1,0:T(8,128)S(1)} all-reduce(f32[10,1024]{1,0:T(8,128)S(1)} %psum.29), channel_id=1, replica_groups=mesh['shard'=8,'tensor'=4,'section'=8] {'section'}, use_global_device_ids=true, to_apply=%region_4.0 | all-reduce | flops 10240 | bytes 81920 | tf_op jit(solution)/shard_map/psum | solution.py:53
  69.7 0.6 multiply_reduce_fusion.1
  70.4 98.8 %reduce-scatter.2.cloned.1.call-done = f32[64,2,256]{2,0,1:T(8,128)} async-done(((f32[4096,2,256]{2,0,1:T(8,128)}), f32[64,2,256]{2,0,1:T(8,128)}) %reduce-scatter.2.cloned.1.call-update) | async-done | bytes 131088 | tf_op jit(solution)/shard_map/reduce_scatter | solution.py:43
  169.2 1.5 multiply_reduce_fusion
  170.7 9.0 %psum.31 = f32[]{:T(128)} all-reduce(f32[]{:T(128)} %multiply_reduce_fusion.1), channel_id=1, replica_groups=mesh['shard'=8,'tensor'=4,'section'=8] {'tensor'}, use_global_device_ids=true, to_apply=%region_6.0 | all-reduce | flops 1 | bytes 8 | tf_op jit(solution)/shard_map/psum | solution.py:55
  179.7 80.5 %psum.28 = f32[]{:T(128)} all-reduce(f32[]{:T(128)} %multiply_reduce_fusion), channel_id=1, replica_groups=mesh['shard'=8,'tensor'=4,'section'=8] {'shard','tensor','section'}, use_global_device_ids=true, to_apply=%region_2.0 | all-reduce | flops 1 | bytes 8 | tf_op jit(solution)/shard_map/psum | solution.py:54
  261.7 1.7 fusion.8
  263.3 0.0 all-gather.2.cloned.1.call-update
  263.4 0.8 copy.23
  264.1 0.8 copy.24
  264.9 0.8 copy.25
  265.7 0.7 fusion.6
  266.4 72.4 %all-gather.2.cloned.1.call-done = bf16[4096,2,256]{2,0,1:T(8,128)(2,1)} async-done(((bf16[64,2,256]{2,0,1:T(8,128)(2,1)}), bf16[4096,2,256]{2,0,1:T(8,128)(2,1)}) %all-gather.2.cloned.1.call-update) | async-done | bytes 4194320 | tf_op jit(solution)/shard_map/all_gather | solution.py:69
  338.8 10.1 %copy.26 = bf16[4096,2,256]{2,1,0:T(2,128)(2,1)} copy(bf16[4096,2,256]{2,0,1:T(8,128)(2,1)} %all-gather.2.cloned.1.call-done) | data formatting | bytes 8388608
  (13 shorter events, 0.0 us)
Async XLA Ops:
  7.2 1.2 copy-start
  7.2 162.0 %reduce-scatter.2.cloned.1.call-start = ((), (), s32[]{:S(2)}) async-start(), calls=%async_computation.1 | async-start | bytes 8519680 | tf_op jit(solution)/shard_map/reduce_scatter | solution.py:43
  18.7 0.8 copy-start.7
  18.7 242.9 %copy-start.1 = (f32[64,2,256]{2,1,0:T(2,128)S(1)}, f32[64,2,256]{2,1,0:T(2,128)}, u32[]{:S(2)}) copy-start(f32[64,2,256]{2,1,0:T(2,128)} %param.12) | copy-start | bytes 393220
  18.7 242.9 %copy-start.2 = (f32[64,2,256]{2,1,0:T(2,128)S(1)}, f32[64,2,256]{2,1,0:T(2,128)}, u32[]{:S(2)}) copy-start(f32[64,2,256]{2,1,0:T(2,128)} %param.13) | copy-start | bytes 393220
  18.8 242.9 %copy-start.3 = (f32[64,2,256]{2,1,0:T(2,128)S(1)}, f32[64,2,256]{2,1,0:T(2,128)}, u32[]{:S(2)}) copy-start(f32[64,2,256]{2,1,0:T(2,128)} %param.14) | copy-start | bytes 393220
  18.8 246.9 %copy-start.4 = (f32[10,1024]{1,0:T(8,128)S(1)}, f32[10,1024]{1,0:T(8,128)}, u32[]{:S(2)}) copy-start(f32[10,1024]{1,0:T(8,128)} %param.15) | copy-start | bytes 122884
  18.8 246.9 %copy-start.5 = (f32[10,1024]{1,0:T(8,128)S(1)}, f32[10,1024]{1,0:T(8,128)}, u32[]{:S(2)}) copy-start(f32[10,1024]{1,0:T(8,128)} %param.16) | copy-start | bytes 122884
  18.8 246.9 %copy-start.6 = (f32[10,1024]{1,0:T(8,128)S(1)}, f32[10,1024]{1,0:T(8,128)}, u32[]{:S(2)}) copy-start(f32[10,1024]{1,0:T(8,128)} %param.17) | copy-start | bytes 122884
  18.8 320.0 %all-gather.2.cloned.1.call-start = ((), (), s32[]{:S(2)}) async-start(), calls=%async_computation.2 | async-start | bytes 4259840 | tf_op jit(solution)/shard_map/all_gather | solution.py:69
Sparse Core Ops, SparseCore 0:
  18.9 150.1 reduce-scatter.1
  263.5 75.2 all-gather.1
